TPU v7x, 1024 devices: a whole 4x8x16 slice. The times are simulated.
1024 devices in a mesh: brick: 64 (over x, y, core), node: 16 (over z).
Axes of the slice: x: 4, y: 8, z: 16, core: 2. Of those that a mesh axis runs over, the one named last changes fastest.
Arguments:
- density: float32 [64, 16, 2, 65536], P('brick', None, None, 'node'), may hold values from -68 to 68
- owner_map: int32 [64, 16], P('brick'), may hold values from 0 to 15, each once within a row
- view_rank: int32 [1024], replicated, may hold values from 0 to 1023, as said below
Outputs:
- image: float32 [4, 16, 4096], P(None, 'node', 'brick')
Inputs may be any that keep to these rules, and one draw needn't show every extreme that they name: view_rank is a permutation: the rank of index i is i with its bit order reversed over the bits of 1023, XOR one drawn number.
All inputs are finite; a program needn't handle non-finite values.
Results may differ from a plain program's by a relative error of at most 0.0003.
Values sent between devices are 32-bit elements; how exact they have to be, the bound alone decides.
No kernel may reach another device: no remote copies, remote signals or barrier semaphores. Data moves between devices by JAX's collectives and lax.ppermute only.
A program may use at most 32 MiB of HBM per device.

v0:
```python
import jax
import jax.numpy as jnp
from jax import lax
from jax.sharding import PartitionSpec as P


def partner_2(value, axis, distance):
    mask = 2**distance
    pairs = [(source, source ^ mask) for source in range(lax.axis_size(axis))]
    return lax.ppermute(value, axis, pairs)


def render(cells, kappa):
    shape = cells.shape[:-2] + cells.shape[-1:]
    red = jnp.zeros(shape, jnp.float32)
    green = jnp.zeros(shape, jnp.float32)
    blue = jnp.zeros(shape, jnp.float32)
    opacity = jnp.zeros(shape, jnp.float32)
    for slab in range(cells.shape[-2]):
        value = cells[..., slab, :]
        square = value * value
        alpha = 1.0 - jnp.exp(-kappa * square)
        weight = (1.0 - opacity) * alpha
        red = red + weight * jnp.exp(-0.125 * (value + 3.0) ** 2)
        green = green + weight * jnp.exp(-0.125 * square)
        blue = blue + weight * jnp.exp(-0.125 * (value - 3.0) ** 2)
        opacity = opacity + weight
    return jnp.stack([red, green, blue, opacity], axis=0)


def over(front, back):
    return front + (1.0 - front[3:4]) * back


def brick_round(picture, brick_index, positions, bit, shift, view_rank):
    half = picture.shape[2] // 2
    lower = picture[:, :, :half]
    upper = picture[:, :, half:]
    upper_side = brick_index >> bit & 1 == 1
    keep = jnp.where(upper_side, upper, lower)
    give = jnp.where(upper_side, lower, upper)
    arrived = partner_2(give, "brick", bit)
    partners = positions ^ 1 << bit + shift
    own_first = (view_rank[positions] < view_rank[partners]).reshape(1, -1, 1)
    return jnp.where(own_first, over(keep, arrived), over(arrived, keep))


def node_round(picture, node_index, position, bit, view_rank):
    half = picture.shape[1] // 2
    lower = picture[:, :half]
    upper = picture[:, half:]
    upper_side = node_index >> bit & 1 == 1
    keep = jnp.where(upper_side, upper, lower)
    give = jnp.where(upper_side, lower, upper)
    arrived = partner_2(give, "node", bit)
    partner = position ^ 1 << bit
    own_first = view_rank[position] < view_rank[partner]
    return jnp.where(own_first, over(keep, arrived), over(arrived, keep))


def composite_own(picture, brick_index, node_index, view_rank):
    nodes = lax.axis_size("node")
    bricks = lax.axis_size("brick")
    node_bits = nodes.bit_length() - 1
    brick_bits = bricks.bit_length() - 1
    position = brick_index * nodes + node_index
    own_slot = jnp.reshape(position, (1,))
    for bit in reversed(range(brick_bits)):
        picture = brick_round(picture, brick_index, own_slot, bit, node_bits, view_rank)
    for bit in reversed(range(node_bits)):
        picture = node_round(picture, node_index, position, bit, view_rank)
    return picture


def shards(density, owner_map, view_rank):
    nodes = lax.axis_size("node")
    bricks = lax.axis_size("brick")
    depth = density.shape[2]
    width = density.shape[3]
    kappa = 2.0 / (depth * bricks * nodes)
    brick_index = lax.axis_index("brick")
    node_index = lax.axis_index("node")
    inverse = jnp.argsort(owner_map[0])
    ordered = jnp.take(density[0], inverse, axis=0)
    brick_cells = lax.all_to_all(ordered, "node", split_axis=0, concat_axis=2, tiled=True)
    picture = render(brick_cells[0], kappa).reshape(4, nodes, width)
    image = composite_own(picture, brick_index, node_index, view_rank)
    return image


def solution(mesh):
    in_specs = (P("brick", None, None, "node"), P("brick", None), P())
    out_specs = P(None, "node", "brick")
    return jax.shard_map(shards, mesh=mesh, in_specs=in_specs, out_specs=out_specs, check_vma=False)
```

profile of v0, /device:TPU:36, one launch (start us, length us, event | category | flops | bytes accessed | tf_op | source)
XLA Modules:
  0.0 148.9 jit_solution(10563449110205247508)
XLA Ops:
  0.7 1.2 sort.17
  2.0 1.1 gather_fusion
  3.1 1.1 broadcast_select_fusion
  4.2 18.9 %all-to-all-start = ((f32[16,2,4096]{2,1,0:T(2,128)}), f32[16,2,4096]{2,1,0:T(2,128)S(1)}, u32[]{:S(2)}, u32[]{:S(2)}) async-start(f32[16,2,4096]{2,1,0:T(2,128)} %broadcast_select_fusion), calls=%async_computation | async-start | bytes 1048576 | tf_op jit(solution)/shard_map/all_to_all | solution.py:85
  23.1 29.1 %all-to-all-done = f32[16,2,4096]{2,1,0:T(2,128)S(1)} async-done(((f32[16,2,4096]{2,1,0:T(2,128)}), f32[16,2,4096]{2,1,0:T(2,128)S(1)}, u32[]{:S(2)}, u32[]{:S(2)}) %all-to-all-start) | async-done | bytes 524320 | tf_op jit(solution)/shard_map/all_to_all | solution.py:85
  53.1 2.4 %collective-permute-start = (f32[4,16,2048]{2,1,0:T(8,128)S(1)}, f32[4,16,2048]{2,1,0:T(8,128)S(1)}, u32[]{:S(2)}, u32[]{:S(2)}) collective-permute-start(f32[4,16,2048]{2,1,0:T(8,128)S(1)} %get-tuple-element.85), channel_id=1, source_target_pairs={{0,512},{16,528},{32,544},{48,560},{64,576},{80,592},{96,608},{112... | collective-permute-start | bytes 1572872 | tf_op jit(solution)/shard_map/ppermute | solution.py:10
  58.2 10.2 %collective-permute-done = f32[4,16,2048]{2,1,0:T(8,128)S(1)} collective-permute-done((f32[4,16,2048]{2,1,0:T(8,128)S(1)}, f32[4,16,2048]{2,1,0:T(8,128)S(1)}, u32[]{:S(2)}, u32[]{:S(2)}) %collective-permute-start) | collective-permute-done | bytes 524320 | tf_op jit(solution)/shard_map/ppermute | solution.py:10
  68.6 3.1 %collective-permute-start.1 = (f32[4,16,1024]{2,1,0:T(8,128)S(1)}, f32[4,16,1024]{2,1,0:T(8,128)S(1)}, u32[]{:S(2)}, u32[]{:S(2)}) collective-permute-start(f32[4,16,1024]{2,1,0:T(8,128)S(1)} %get-tuple-element.87), channel_id=1, source_target_pairs={{0,256},{16,272},{32,288},{48,304},{64,320},{80,336},{96,352},{112... | collective-permute-start | bytes 786440 | tf_op jit(solution)/shard_map/ppermute | solution.py:10
  83.1 2.0 %collective-permute-start.2 = (f32[4,16,512]{2,1,0:T(8,128)S(1)}, f32[4,16,512]{2,1,0:T(8,128)S(1)}, u32[]{:S(2)}, u32[]{:S(2)}) collective-permute-start(f32[4,16,512]{2,1,0:T(8,128)S(1)} %get-tuple-element.93), channel_id=1, source_target_pairs={{0,128},{16,144},{32,160},{48,176},{64,192},{80,208},{96,224},{112... | collective-permute-start | bytes 393224 | tf_op jit(solution)/shard_map/ppermute | solution.py:10
  85.1 10.4 %collective-permute-done.2 = f32[4,16,512]{2,1,0:T(8,128)S(1)} collective-permute-done((f32[4,16,512]{2,1,0:T(8,128)S(1)}, f32[4,16,512]{2,1,0:T(8,128)S(1)}, u32[]{:S(2)}, u32[]{:S(2)}) %collective-permute-start.2) | collective-permute-done | bytes 131104 | tf_op jit(solution)/shard_map/ppermute | solution.py:10
  95.5 1.9 %collective-permute-start.3 = (f32[4,16,256]{2,1,0:T(8,128)S(1)}, f32[4,16,256]{2,1,0:T(8,128)S(1)}, u32[]{:S(2)}, u32[]{:S(2)}) collective-permute-start(f32[4,16,256]{2,1,0:T(8,128)S(1)} %get-tuple-element.95), channel_id=1, source_target_pairs={{0,64},{16,80},{32,96},{48,112},{64,0},{80,16},{96,32},{112,48},{1... | collective-permute-start | bytes 196616 | tf_op jit(solution)/shard_map/ppermute | solution.py:10
  97.5 5.8 %collective-permute-done.3 = f32[4,16,256]{2,1,0:T(8,128)S(1)} collective-permute-done((f32[4,16,256]{2,1,0:T(8,128)S(1)}, f32[4,16,256]{2,1,0:T(8,128)S(1)}, u32[]{:S(2)}, u32[]{:S(2)}) %collective-permute-start.3) | collective-permute-done | bytes 65568 | tf_op jit(solution)/shard_map/ppermute | solution.py:10
  103.3 2.1 %collective-permute-start.4 = (f32[4,16,128]{2,1,0:T(8,128)S(1)}, f32[4,16,128]{2,1,0:T(8,128)S(1)}, u32[]{:S(2)}, u32[]{:S(2)}) collective-permute-start(f32[4,16,128]{2,1,0:T(8,128)S(1)} %get-tuple-element.97), channel_id=1, source_target_pairs={{0,32},{16,48},{32,0},{48,16},{64,96},{80,112},{96,64},{112,80},{1... | collective-permute-start | bytes 98312 | tf_op jit(solution)/shard_map/ppermute | solution.py:10
  105.5 3.7 %collective-permute-done.4 = f32[4,16,128]{2,1,0:T(8,128)S(1)} collective-permute-done((f32[4,16,128]{2,1,0:T(8,128)S(1)}, f32[4,16,128]{2,1,0:T(8,128)S(1)}, u32[]{:S(2)}, u32[]{:S(2)}) %collective-permute-start.4) | collective-permute-done | bytes 32800 | tf_op jit(solution)/shard_map/ppermute | solution.py:10
  109.2 1.9 %collective-permute-start.5 = (f32[4,16,64]{2,1,0:T(8,128)S(1)}, f32[4,16,64]{2,1,0:T(8,128)S(1)}, u32[]{:S(2)}, u32[]{:S(2)}) collective-permute-start(f32[4,16,64]{2,1,0:T(8,128)S(1)} %get-tuple-element.101), channel_id=1, source_target_pairs={{0,16},{16,0},{32,48},{48,32},{64,80},{80,64},{96,112},{112,96},{1... | collective-permute-start | bytes 49160 | tf_op jit(solution)/shard_map/ppermute | solution.py:10
  111.2 1.2 collective-permute-done.5
  112.4 9.0 %collective-permute-start.6 = (f32[4,8,64]{2,1,0:T(8,128)S(1)}, f32[4,8,64]{2,1,0:T(8,128)S(1)}, u32[]{:S(2)}, u32[]{:S(2)}) collective-permute-start(f32[4,8,64]{2,1,0:T(8,128)S(1)} %get-tuple-element.99), channel_id=1, source_target_pairs={{0,8},{1,9},{2,10},{3,11},{4,12},{5,13},{6,14},{7,15},{8,0},{9,1},... | collective-permute-start | bytes 24584 | tf_op jit(solution)/shard_map/ppermute | solution.py:10
  121.4 5.5 %collective-permute-done.6 = f32[4,8,64]{2,1,0:T(8,128)S(1)} collective-permute-done((f32[4,8,64]{2,1,0:T(8,128)S(1)}, f32[4,8,64]{2,1,0:T(8,128)S(1)}, u32[]{:S(2)}, u32[]{:S(2)}) %collective-permute-start.6) | collective-permute-done | bytes 8224 | tf_op jit(solution)/shard_map/ppermute | solution.py:10
  126.9 3.9 %collective-permute-start.7 = (f32[4,4,64]{2,1,0:T(4,128)S(1)}, f32[4,4,64]{2,1,0:T(4,128)S(1)}, u32[]{:S(2)}, u32[]{:S(2)}) collective-permute-start(f32[4,4,64]{2,1,0:T(4,128)S(1)} %get-tuple-element.103), channel_id=1, source_target_pairs={{0,4},{1,5},{2,6},{3,7},{4,0},{5,1},{6,2},{7,3},{8,12},{9,13},{10,... | collective-permute-start | bytes 12296 | tf_op jit(solution)/shard_map/ppermute | solution.py:10
  130.8 5.6 %collective-permute-done.7 = f32[4,4,64]{2,1,0:T(4,128)S(1)} collective-permute-done((f32[4,4,64]{2,1,0:T(4,128)S(1)}, f32[4,4,64]{2,1,0:T(4,128)S(1)}, u32[]{:S(2)}, u32[]{:S(2)}) %collective-permute-start.7) | collective-permute-done | bytes 4128 | tf_op jit(solution)/shard_map/ppermute | solution.py:10
  136.4 1.9 %collective-permute-start.8 = (f32[4,2,64]{2,1,0:T(2,128)S(1)}, f32[4,2,64]{2,1,0:T(2,128)S(1)}, u32[]{:S(2)}, u32[]{:S(2)}) collective-permute-start(f32[4,2,64]{2,1,0:T(2,128)S(1)} %get-tuple-element.105), channel_id=1, source_target_pairs={{0,2},{1,3},{2,0},{3,1},{4,6},{5,7},{6,4},{7,5},{8,10},{9,11},{10,... | collective-permute-start | bytes 6152 | tf_op jit(solution)/shard_map/ppermute | solution.py:10
  138.3 4.5 %collective-permute-done.8 = f32[4,2,64]{2,1,0:T(2,128)S(1)} collective-permute-done((f32[4,2,64]{2,1,0:T(2,128)S(1)}, f32[4,2,64]{2,1,0:T(2,128)S(1)}, u32[]{:S(2)}, u32[]{:S(2)}) %collective-permute-start.8) | collective-permute-done | bytes 2080 | tf_op jit(solution)/shard_map/ppermute | solution.py:10
  142.9 1.9 %collective-permute-start.9 = (f32[4,1,64]{2,1,0:T(1,128)S(1)}, f32[4,1,64]{2,1,0:T(1,128)S(1)}, u32[]{:S(2)}, u32[]{:S(2)}) collective-permute-start(f32[4,1,64]{2,1,0:T(1,128)S(1)} %get-tuple-element.107), channel_id=1, source_target_pairs={{0,1},{1,0},{2,3},{3,2},{4,5},{5,4},{6,7},{7,6},{8,9},{9,8},{10,11... | collective-permute-start | bytes 3080 | tf_op jit(solution)/shard_map/ppermute | solution.py:10
  144.8 3.5 %collective-permute-done.9 = f32[4,1,64]{2,1,0:T(1,128)S(1)} collective-permute-done((f32[4,1,64]{2,1,0:T(1,128)S(1)}, f32[4,1,64]{2,1,0:T(1,128)S(1)}, u32[]{:S(2)}, u32[]{:S(2)}) %collective-permute-start.9) | collective-permute-done | bytes 1056 | tf_op jit(solution)/shard_map/ppermute | solution.py:10
  (59 shorter events, 4.1 us)
Async XLA Ops:
  0.0 2.0 %copy-start = (f32[1,16,2,4096]{3,2,1,0:T(2,128)S(1)}, f32[1,16,2,4096]{3,2,1,0:T(2,128)}, u32[]{:S(2)}) copy-start(f32[1,16,2,4096]{3,2,1,0:T(2,128)} %param.3) | copy-start | bytes 1572868
  0.0 0.7 copy-start.2
  4.2 47.9 %all-to-all-start = ((f32[16,2,4096]{2,1,0:T(2,128)}), f32[16,2,4096]{2,1,0:T(2,128)S(1)}, u32[]{:S(2)}, u32[]{:S(2)}) async-start(f32[16,2,4096]{2,1,0:T(2,128)} %broadcast_select_fusion), calls=%async_computation | async-start | bytes 1048576 | tf_op jit(solution)/shard_map/all_to_all | solution.py:85
  53.1 15.4 %collective-permute-start = (f32[4,16,2048]{2,1,0:T(8,128)S(1)}, f32[4,16,2048]{2,1,0:T(8,128)S(1)}, u32[]{:S(2)}, u32[]{:S(2)}) collective-permute-start(f32[4,16,2048]{2,1,0:T(8,128)S(1)} %get-tuple-element.85), channel_id=1, source_target_pairs={{0,512},{16,528},{32,544},{48,560},{64,576},{80,592},{96,608},{112... | collective-permute-start | bytes 1572872 | tf_op jit(solution)/shard_map/ppermute | solution.py:10
  55.6 0.7 copy-start.1
  68.6 14.3 %collective-permute-start.1 = (f32[4,16,1024]{2,1,0:T(8,128)S(1)}, f32[4,16,1024]{2,1,0:T(8,128)S(1)}, u32[]{:S(2)}, u32[]{:S(2)}) collective-permute-start(f32[4,16,1024]{2,1,0:T(8,128)S(1)} %get-tuple-element.87), channel_id=1, source_target_pairs={{0,256},{16,272},{32,288},{48,304},{64,320},{80,336},{96,352},{112... | collective-permute-start | bytes 786440 | tf_op jit(solution)/shard_map/ppermute | solution.py:10
  83.1 12.4 %collective-permute-start.2 = (f32[4,16,512]{2,1,0:T(8,128)S(1)}, f32[4,16,512]{2,1,0:T(8,128)S(1)}, u32[]{:S(2)}, u32[]{:S(2)}) collective-permute-start(f32[4,16,512]{2,1,0:T(8,128)S(1)} %get-tuple-element.93), channel_id=1, source_target_pairs={{0,128},{16,144},{32,160},{48,176},{64,192},{80,208},{96,224},{112... | collective-permute-start | bytes 393224 | tf_op jit(solution)/shard_map/ppermute | solution.py:10
  95.5 7.8 %collective-permute-start.3 = (f32[4,16,256]{2,1,0:T(8,128)S(1)}, f32[4,16,256]{2,1,0:T(8,128)S(1)}, u32[]{:S(2)}, u32[]{:S(2)}) collective-permute-start(f32[4,16,256]{2,1,0:T(8,128)S(1)} %get-tuple-element.95), channel_id=1, source_target_pairs={{0,64},{16,80},{32,96},{48,112},{64,0},{80,16},{96,32},{112,48},{1... | collective-permute-start | bytes 196616 | tf_op jit(solution)/shard_map/ppermute | solution.py:10
  103.3 5.8 %collective-permute-start.4 = (f32[4,16,128]{2,1,0:T(8,128)S(1)}, f32[4,16,128]{2,1,0:T(8,128)S(1)}, u32[]{:S(2)}, u32[]{:S(2)}) collective-permute-start(f32[4,16,128]{2,1,0:T(8,128)S(1)} %get-tuple-element.97), channel_id=1, source_target_pairs={{0,32},{16,48},{32,0},{48,16},{64,96},{80,112},{96,64},{112,80},{1... | collective-permute-start | bytes 98312 | tf_op jit(solution)/shard_map/ppermute | solution.py:10
  109.2 3.1 %collective-permute-start.5 = (f32[4,16,64]{2,1,0:T(8,128)S(1)}, f32[4,16,64]{2,1,0:T(8,128)S(1)}, u32[]{:S(2)}, u32[]{:S(2)}) collective-permute-start(f32[4,16,64]{2,1,0:T(8,128)S(1)} %get-tuple-element.101), channel_id=1, source_target_pairs={{0,16},{16,0},{32,48},{48,32},{64,80},{80,64},{96,112},{112,96},{1... | collective-permute-start | bytes 49160 | tf_op jit(solution)/shard_map/ppermute | solution.py:10
  112.4 14.5 %collective-permute-start.6 = (f32[4,8,64]{2,1,0:T(8,128)S(1)}, f32[4,8,64]{2,1,0:T(8,128)S(1)}, u32[]{:S(2)}, u32[]{:S(2)}) collective-permute-start(f32[4,8,64]{2,1,0:T(8,128)S(1)} %get-tuple-element.99), channel_id=1, source_target_pairs={{0,8},{1,9},{2,10},{3,11},{4,12},{5,13},{6,14},{7,15},{8,0},{9,1},... | collective-permute-start | bytes 24584 | tf_op jit(solution)/shard_map/ppermute | solution.py:10
  126.9 9.5 %collective-permute-start.7 = (f32[4,4,64]{2,1,0:T(4,128)S(1)}, f32[4,4,64]{2,1,0:T(4,128)S(1)}, u32[]{:S(2)}, u32[]{:S(2)}) collective-permute-start(f32[4,4,64]{2,1,0:T(4,128)S(1)} %get-tuple-element.103), channel_id=1, source_target_pairs={{0,4},{1,5},{2,6},{3,7},{4,0},{5,1},{6,2},{7,3},{8,12},{9,13},{10,... | collective-permute-start | bytes 12296 | tf_op jit(solution)/shard_map/ppermute | solution.py:10
  136.4 6.4 %collective-permute-start.8 = (f32[4,2,64]{2,1,0:T(2,128)S(1)}, f32[4,2,64]{2,1,0:T(2,128)S(1)}, u32[]{:S(2)}, u32[]{:S(2)}) collective-permute-start(f32[4,2,64]{2,1,0:T(2,128)S(1)} %get-tuple-element.105), channel_id=1, source_target_pairs={{0,2},{1,3},{2,0},{3,1},{4,6},{5,7},{6,4},{7,5},{8,10},{9,11},{10,... | collective-permute-start | bytes 6152 | tf_op jit(solution)/shard_map/ppermute | solution.py:10
  142.9 5.5 %collective-permute-start.9 = (f32[4,1,64]{2,1,0:T(1,128)S(1)}, f32[4,1,64]{2,1,0:T(1,128)S(1)}, u32[]{:S(2)}, u32[]{:S(2)}) collective-permute-start(f32[4,1,64]{2,1,0:T(1,128)S(1)} %get-tuple-element.107), channel_id=1, source_target_pairs={{0,1},{1,0},{2,3},{3,2},{4,5},{5,4},{6,7},{7,6},{8,9},{9,8},{10,11... | collective-permute-start | bytes 3080 | tf_op jit(solution)/shard_map/ppermute | solution.py:10
where the time goes:
time: 150 us; the launch traced here: 149 us
  waiting for transfers between devices  79.4 us (53%)
  starting transfers between devices  49 us (33%)
  between operations  12.9 us (9%)
  other arithmetic  4.07 us (3%)
  local copies, waits for them, and re-layouts  3.53 us (2%)
    ppermute x10, waiting for transfers between devices, partner_2(): return lax.ppermute(value, axis, pairs)  50.3 us
    ppermute x10, starting transfers between devices, partner_2(): return lax.ppermute(value, axis, pairs)  30.2 us
    all_to_all x1, waiting for transfers between devices, shards(): lax.all_to_all(ordered, 'node', split_axis=0, concat_axis=2, tiled=True)  29.1 us
    all_to_all x1, starting transfers between devices, shards(): lax.all_to_all(ordered, 'node', split_axis=0, concat_axis=2, tiled=True)  18.9 us
  transfers between devices with their start and end apart: 11, of which 10 were waited for; matrix products, arithmetic and copies ran while one was open for 1% of the time, Pallas kernels for 0%

commit v1 on v0

v1 whole, which is shorter than its diff:
```python
import functools
import jax
import jax.numpy as jnp
from jax import lax
from jax.experimental import pallas as pl
from jax.experimental.pallas import tpu as pltpu
from jax.sharding import PartitionSpec as P

LANES = 128
VMEM = pl.BlockSpec(memory_space=pltpu.VMEM)
SMEM = pl.BlockSpec(memory_space=pltpu.SMEM)


def over(front, back):
    keep = front[3]
    return tuple(front[k] + keep * back[k] for k in range(3)) + (keep * back[3],)


def pack_kernel(owner_ref, cells_ref, out_ref):
    bricks, depth, width = cells_ref.shape
    for brick in range(bricks):
        slot = owner_ref[0, brick]
        for slab in range(depth):
            for part in range(width // LANES):
                out_ref[part, pl.ds(slab * bricks + slot, 1), :] = cells_ref[brick, pl.ds(slab, 1), part * LANES:(part + 1) * LANES]


def pack(owner_map, cells):
    bricks, depth, width = cells.shape
    out = jax.ShapeDtypeStruct((width // LANES, depth * bricks, LANES), jnp.float32)
    return pl.pallas_call(pack_kernel, out_shape=out, in_specs=[SMEM, VMEM], out_specs=VMEM, name="pack", compiler_params=pltpu.CompilerParams(vmem_limit_bytes=4 << 20))(owner_map, cells)


def reverse(value, bits):
    return sum((value >> bit & 1) << (bits - 1 - bit) for bit in range(bits))


def composite_kernel(kappa, flip_ref, cells_ref, out_ref):
    chips, rows, lanes = cells_ref.shape
    nodes = out_ref.shape[1]
    depth = rows // nodes
    bits = chips.bit_length() - 1
    flip = flip_ref[0]
    swap = reverse(flip & (chips - 1), bits)
    red = jnp.zeros((nodes, lanes), jnp.float32)
    green = red
    blue = red
    keep = jnp.ones((nodes, lanes), jnp.float32)
    for rank in range(chips):
        chip = reverse(rank, bits) ^ swap
        for slab in range(depth):
            value = cells_ref[chip, slab * nodes:(slab + 1) * nodes, :]
            square = value * value
            alpha = 1.0 - jnp.exp(-kappa * square)
            weight = keep * alpha
            red = red + weight * jnp.exp(-0.125 * (value + 3.0) ** 2)
            green = green + weight * jnp.exp(-0.125 * square)
            blue = blue + weight * jnp.exp(-0.125 * (value - 3.0) ** 2)
            keep = keep - weight
    out_ref[0] = red
    out_ref[1] = green
    out_ref[2] = blue
    out_ref[3] = keep


def composite(cells, flip, nodes, kappa):
    out = jax.ShapeDtypeStruct((4, nodes, cells.shape[2]), jnp.float32)
    return pl.pallas_call(functools.partial(composite_kernel, kappa), out_shape=out, in_specs=[SMEM, VMEM], out_specs=VMEM, name="composite", compiler_params=pltpu.CompilerParams(vmem_limit_bytes=4 << 20))(flip, cells)


def finish_kernel(bits, flip_ref, side_ref, mine_ref, other_ref, out_ref):
    nodes, lanes = mine_ref.shape[1:]
    flip = flip_ref[0]
    side = side_ref[0]
    node_bits = nodes.bit_length() - 1
    mine = tuple(mine_ref[k] for k in range(4))
    other = tuple(other_ref[k] for k in range(4))
    first = (flip >> (bits - 1 - node_bits) & 1) == side
    front = tuple(jnp.where(first, a, b) for a, b in zip(mine, other))
    back = tuple(jnp.where(first, b, a) for a, b in zip(mine, other))
    total = over(front, back)
    row = lax.broadcasted_iota(jnp.int32, (nodes, lanes), 0)
    for bit in reversed(range(node_bits)):
        moved = tuple(pltpu.roll(a, 1 << bit, 0) for a in total) if 2 << bit == nodes else tuple(
            jnp.where((row >> bit & 1) == 0, pltpu.roll(a, nodes - (1 << bit), 0), pltpu.roll(a, 1 << bit, 0)) for a in total)
        ahead = (row >> bit & 1) == (flip >> (bits - 1 - bit) & 1)
        front = tuple(jnp.where(ahead, a, b) for a, b in zip(total, moved))
        back = tuple(jnp.where(ahead, b, a) for a, b in zip(total, moved))
        total = over(front, back)
    half = lanes // 2
    for k in range(4):
        line = total[k][:1] if k < 3 else 1.0 - total[k][:1]
        out_ref[k] = jnp.where(side == 0, line[:, :half], line[:, half:])


def finish(mine, other, flip, side, bits):
    out = jax.ShapeDtypeStruct((4, 1, mine.shape[2] // 2), jnp.float32)
    return pl.pallas_call(functools.partial(finish_kernel, bits), out_shape=out, in_specs=[SMEM, SMEM, VMEM, VMEM], out_specs=VMEM, name="finish", compiler_params=pltpu.CompilerParams(vmem_limit_bytes=4 << 20))(flip, side, mine, other)


def shards(density, owner_map, view_rank):
    nodes = lax.axis_size("node")
    bricks = lax.axis_size("brick")
    kappa = 2.0 / (density.shape[2] * bricks * nodes)
    bits = (bricks * nodes).bit_length() - 1
    same_core = [[2 * chip + core for chip in range(bricks // 2)] for core in range(2)]
    flip = view_rank[:1]
    side = (lax.axis_index("brick") & 1).reshape(1)
    packed = pack(owner_map, density[0])
    cells = lax.all_to_all(packed, "brick", 0, 0, axis_index_groups=same_core, tiled=True)
    mine = composite(cells, flip, nodes, kappa)
    other = lax.ppermute(mine, "brick", [(source, source ^ 1) for source in range(bricks)])
    return finish(mine, other, flip, side, bits)


def solution(mesh):
    in_specs = (P("brick", None, None, "node"), P("brick", None), P())
    out_specs = P(None, "node", "brick")
    return jax.shard_map(shards, mesh=mesh, in_specs=in_specs, out_specs=out_specs, check_vma=False)
```

time: 150 us -> 40.2 us (0.27)
  the two profiles are of different devices: /device:TPU:36 before, /device:TPU:9 now
where the time goes in v1:
time: 40.2 us; the launch traced here: 39.9 us
  starting transfers between devices  20.1 us (50%)
  waiting for transfers between devices  12.3 us (31%)
  Pallas kernels  4.41 us (11%)
  local copies, waits for them, and re-layouts  2.96 us (7%)
    all_to_all x1, waiting for transfers between devices, shards(): lax.all_to_all(packed, 'brick', 0, 0, axis_index_groups=same_core, tiled=...  11.5 us
    ppermute x1, starting transfers between devices, shards(): lax.ppermute(mine, 'brick', [(source, source ^ 1) for source in range(bri...  10.5 us
    all_to_all x1, starting transfers between devices, shards(): lax.all_to_all(packed, 'brick', 0, 0, axis_index_groups=same_core, tiled=...  9.6 us
    pallas_call x1, Pallas kernels, pack(): pl.pallas_call(pack_kernel, out_shape=out, in_specs=[SMEM, VMEM], out_spe...  1.92 us
    unnamed x4, local copies, waits for them, and re-layouts  1.7 us
    pallas_call x1, Pallas kernels, finish(): pl.pallas_call(functools.partial(finish_kernel, bits), out_shape=out, in_...  1.36 us
    slice x1, local copies, waits for them, and re-layouts, shards(): flip = view_rank[:1]  1.26 us
    pallas_call x1, Pallas kernels, composite(): pl.pallas_call(functools.partial(composite_kernel, kappa), out_shape=out,...  1.13 us
  transfers between devices with their start and end apart: 2, of which 2 were waited for; matrix products, arithmetic and copies ran while one was open for 3% of the time, Pallas kernels for 0%

profile of v1, /device:TPU:9, one launch (start us, length us, event | category | flops | bytes accessed | tf_op | source)
XLA Modules:
  0.0 39.9 jit_solution(10236433099713249128)
XLA Ops:
  0.0 0.0 copy-start.1
  0.0 0.7 %copy-done.1 = s32[1,16]{1,0:T(1,128)S(1)} copy-done((s32[1,16]{1,0:T(1,128)S(1)}, s32[1,16]{1,0:T(1,128)}, u32[]{:S(2)}) %copy-start.1) | copy-done | bytes 88
  0.7 0.0 copy-start
  0.7 1.0 %copy-done = f32[1,16,2,4096]{3,2,1,0:T(2,128)S(1)} copy-done((f32[1,16,2,4096]{3,2,1,0:T(2,128)S(1)}, f32[1,16,2,4096]{3,2,1,0:T(2,128)}, u32[]{:S(2)}) %copy-start) | copy-done | bytes 524312
  1.7 1.9 %pack.1 = f32[32,32,128]{2,1,0:T(8,128)} custom-call(s32[1,16]{1,0:T(1,128)S(1)} %copy-done.1, f32[16,2,4096]{2,1,0:T(2,128)S(1)} %bitcast.2), custom_call_target="tpu_custom_call" | custom-call | tf_op jit(solution)/shard_map/pack/pallas_call | solution.py:31
  3.6 9.6 %all-to-all-start = ((f32[32,32,128]{2,1,0:T(8,128)}), f32[32,32,128]{2,1,0:T(8,128)S(1)}, u32[]{:S(2)}, u32[]{:S(2)}) async-start(f32[32,32,128]{2,1,0:T(8,128)} %pack.1), calls=%async_computation | async-start | bytes 1048576 | tf_op jit(solution)/shard_map/all_to_all | solution.py:110
  13.2 1.3 %slice.3.flip_ref = s32[1]{0:T(128)} slice(s32[1024]{0:T(1024)} %param.5), slice={[0:1]} | slice | bytes 8 | tf_op jit(solution)/shard_map/slice | solution.py:107
  14.5 11.5 %all-to-all-done.cells_ref = f32[32,32,128]{2,1,0:T(8,128)S(1)} async-done(((f32[32,32,128]{2,1,0:T(8,128)}), f32[32,32,128]{2,1,0:T(8,128)S(1)}, u32[]{:S(2)}, u32[]{:S(2)}) %all-to-all-start) | async-done | bytes 524320 | tf_op jit(solution)/shard_map/all_to_all | solution.py:110
  26.0 1.1 %composite.1.mine_ref = f32[4,16,128]{2,1,0:T(8,128)S(1)} custom-call(s32[1]{0:T(128)} %slice.3.flip_ref, f32[32,32,128]{2,1,0:T(8,128)S(1)} %all-to-all-done.cells_ref), custom_call_target="tpu_custom_call" | custom-call | tf_op jit(solution)/shard_map/composite/pallas_call | solution.py:68
  27.1 10.5 %collective-permute-start = (f32[4,16,128]{2,1,0:T(8,128)S(1)}, f32[4,16,128]{2,1,0:T(8,128)S(1)}, u32[]{:S(2)}, u32[]{:S(2)}) collective-permute-start(f32[4,16,128]{2,1,0:T(8,128)S(1)} %composite.1.mine_ref), channel_id=1, source_target_pairs={{0,16},{16,0},{32,48},{48,32},{64,80},{80,64},{96,112},{112,96},{1... | collective-permute-start | bytes 98312 | tf_op jit(solution)/shard_map/ppermute | solution.py:112
  37.7 0.8 %collective-permute-done.other_ref = f32[4,16,128]{2,1,0:T(8,128)S(1)} collective-permute-done((f32[4,16,128]{2,1,0:T(8,128)S(1)}, f32[4,16,128]{2,1,0:T(8,128)S(1)}, u32[]{:S(2)}, u32[]{:S(2)}) %collective-permute-start) | collective-permute-done | bytes 32800 | tf_op jit(solution)/shard_map/ppermute | solution.py:112
  38.5 1.4 %finish.1 = f32[4,1,64]{2,1,0:T(1,128)} custom-call(s32[1]{0:T(128)} %slice.3.flip_ref, s32[1]{0:T(128)} %bitcast.side_ref, f32[4,16,128]{2,1,0:T(8,128)S(1)} %composite.1.mine_ref, f32[4,16,128]{2,1,0:T(8,128)S(1)} %collective-permute-done.other_ref), custom_call_target="tpu_custom_call" | custom-call | tf_op jit(solution)/shard_map/finish/pallas_call | solution.py:98
Async XLA Ops:
  0.0 0.7 %copy-start.1 = (s32[1,16]{1,0:T(1,128)S(1)}, s32[1,16]{1,0:T(1,128)}, u32[]{:S(2)}) copy-start(s32[1,16]{1,0:T(1,128)} %owner_ref.1) | copy-start | bytes 196
  0.7 1.0 %copy-start = (f32[1,16,2,4096]{3,2,1,0:T(2,128)S(1)}, f32[1,16,2,4096]{3,2,1,0:T(2,128)}, u32[]{:S(2)}) copy-start(f32[1,16,2,4096]{3,2,1,0:T(2,128)} %param.3) | copy-start | bytes 1572868
  3.6 22.4 %all-to-all-start = ((f32[32,32,128]{2,1,0:T(8,128)}), f32[32,32,128]{2,1,0:T(8,128)S(1)}, u32[]{:S(2)}, u32[]{:S(2)}) async-start(f32[32,32,128]{2,1,0:T(8,128)} %pack.1), calls=%async_computation | async-start | bytes 1048576 | tf_op jit(solution)/shard_map/all_to_all | solution.py:110
  27.1 11.4 %collective-permute-start = (f32[4,16,128]{2,1,0:T(8,128)S(1)}, f32[4,16,128]{2,1,0:T(8,128)S(1)}, u32[]{:S(2)}, u32[]{:S(2)}) collective-permute-start(f32[4,16,128]{2,1,0:T(8,128)S(1)} %composite.1.mine_ref), channel_id=1, source_target_pairs={{0,16},{16,0},{32,48},{48,32},{64,80},{80,64},{96,112},{112,96},{1... | collective-permute-start | bytes 98312 | tf_op jit(solution)/shard_map/ppermute | solution.py:112

commit v2 on v1

v2 whole, which is shorter than its diff:
```python
import functools
import math
import jax
import jax.numpy as jnp
from jax import lax
from jax.experimental import pallas as pl
from jax.experimental.pallas import tpu as pltpu
from jax.sharding import PartitionSpec as P

LANES = 128
VMEM = pl.BlockSpec(memory_space=pltpu.VMEM)
SMEM = pl.BlockSpec(memory_space=pltpu.SMEM)
HBM = pl.BlockSpec(memory_space=pltpu.HBM)
PARAMS = pltpu.CompilerParams(vmem_limit_bytes=4 << 20)


def over(front, back):
    keep = front[3]
    return tuple(front[k] + keep * back[k] for k in range(3)) + (keep * back[3],)


def pack_kernel(owner_hbm, cells_hbm, out_ref, owner_ref, owner_sem, sems):
    bricks = cells_hbm.shape[0]
    fetch = pltpu.make_async_copy(owner_hbm, owner_ref, owner_sem)
    fetch.start()
    fetch.wait()
    copies = [pltpu.make_async_copy(cells_hbm.at[brick], out_ref.at[:, owner_ref[0, brick]], sems.at[brick]) for brick in range(bricks)]
    for copy in copies:
        copy.start()
    for copy in copies:
        copy.wait()


def pack(owner_map, cells):
    bricks, depth, width = cells.shape
    parts = width // LANES
    tiles = cells.reshape(bricks, depth, parts, LANES).transpose(0, 2, 1, 3)
    return pl.pallas_call(
        pack_kernel,
        out_shape=pltpu.VMEM((parts, bricks, depth, LANES), jnp.float32),
        in_specs=[HBM, HBM],
        out_specs=VMEM,
        scratch_shapes=[pltpu.SMEM((1, bricks), jnp.int32), pltpu.SemaphoreType.DMA, pltpu.SemaphoreType.DMA((bricks,))],
        compiler_params=PARAMS,
        name="pack",
    )(pltpu.with_memory_space_constraint(owner_map, pltpu.HBM), pltpu.with_memory_space_constraint(tiles, pltpu.HBM))


def reverse(value, bits):
    return sum((value >> bit & 1) << (bits - 1 - bit) for bit in range(bits))


def composite_kernel(kappa, depth, flip_ref, cells_ref, out_ref):
    chips, rows, lanes = cells_ref.shape
    nodes = rows // depth
    bits = chips.bit_length() - 1
    swap = reverse(flip_ref[0] & (chips - 1), bits)
    scale = -0.125 * math.log2(math.e)
    red = jnp.zeros((nodes, lanes), jnp.float32)
    green = red
    blue = red
    keep = jnp.ones((nodes, lanes), jnp.float32)
    for rank in range(chips):
        chip = reverse(rank, bits) ^ swap
        for slab in range(depth):
            value = cells_ref[chip, pl.ds(slab, nodes, stride=depth), :]
            middle = value * value * scale
            slope = value * (6.0 * scale)
            side = middle + 9.0 * scale
            rest = keep * jnp.exp2(middle * (8.0 * kappa))
            weight = keep - rest
            red = red + weight * jnp.exp2(side + slope)
            green = green + weight * jnp.exp2(middle)
            blue = blue + weight * jnp.exp2(side - slope)
            keep = rest
    out_ref[0] = red
    out_ref[1] = green
    out_ref[2] = blue
    out_ref[3] = keep


def composite(cells, flip, kappa):
    chips, nodes, depth, lanes = cells.shape
    return pl.pallas_call(
        functools.partial(composite_kernel, kappa, depth),
        out_shape=pltpu.VMEM((4, nodes, lanes), jnp.float32),
        in_specs=[SMEM, VMEM],
        out_specs=VMEM,
        compiler_params=PARAMS,
        name="composite",
    )(flip, cells.reshape(chips, nodes * depth, lanes))


def finish_kernel(bits, flip_ref, side_ref, parts_ref, out_ref):
    nodes, lanes = parts_ref.shape[2:]
    flip = flip_ref[0]
    node_bits = nodes.bit_length() - 1
    ahead = flip >> (bits - 1 - node_bits) & 1
    total = over(tuple(parts_ref[ahead, k] for k in range(4)), tuple(parts_ref[1 - ahead, k] for k in range(4)))
    for bit in reversed(range(node_bits)):
        half = 1 << bit
        low = tuple(a[:half] for a in total)
        high = tuple(a[half:] for a in total)
        ahead = (flip >> (bits - 1 - bit) & 1) == 0
        front = tuple(jnp.where(ahead, a, b) for a, b in zip(low, high))
        back = tuple(jnp.where(ahead, b, a) for a, b in zip(low, high))
        total = over(front, back)
    first = side_ref[0] == 0
    for k in range(4):
        line = total[k] if k < 3 else 1.0 - total[k]
        out_ref[k] = jnp.where(first, line[:, :lanes // 2], line[:, lanes // 2:])


def finish(parts, flip, side, bits):
    out = pltpu.VMEM((4, 1, parts.shape[3] // 2), jnp.float32)
    return pl.pallas_call(functools.partial(finish_kernel, bits), out_shape=out, in_specs=[SMEM, SMEM, VMEM], out_specs=VMEM, compiler_params=PARAMS, name="finish")(flip, side, parts)


def shards(density, owner_map, view_rank):
    nodes = lax.axis_size("node")
    bricks = lax.axis_size("brick")
    kappa = 2.0 / (density.shape[2] * bricks * nodes)
    bits = (bricks * nodes).bit_length() - 1
    same_core = [[2 * chip + core for chip in range(bricks // 2)] for core in range(2)]
    same_chip = [[2 * chip, 2 * chip + 1] for chip in range(bricks // 2)]
    flip = view_rank[:1]
    side = (lax.axis_index("brick") & 1).reshape(1)
    packed = pack(owner_map, density[0])
    cells = lax.all_to_all(packed, "brick", 0, 0, axis_index_groups=same_core, tiled=True)
    mine = composite(cells, flip, kappa)
    both = lax.all_gather(mine, "brick", axis_index_groups=same_chip)
    return finish(both, flip, side, bits)


def solution(mesh):
    in_specs = (P("brick", None, None, "node"), P("brick", None), P())
    out_specs = P(None, "node", "brick")
    return jax.shard_map(shards, mesh=mesh, in_specs=in_specs, out_specs=out_specs, check_vma=False)
```

time: 40.2 us -> 37.8 us (0.940)
  starting transfers between devices: 20.1 us -> 9.62 us
  blocking collectives: 0 us -> 10.1 us
  local copies, waits for them, and re-layouts: 2.96 us -> 1.78 us
  waiting for transfers between devices: 12.3 us -> 11.5 us
    ppermute x1 -> x0, starting transfers between devices: 10.5 us -> none  [shards(): lax.ppermute(mine, 'brick', [(source, source ^ 1) for source in range(bri...]
    all_gather x0 -> x1, blocking collectives: none -> 10.1 us  [shards(): both = lax.all_gather(mine, 'brick', axis_index_groups=same_chip)]
    unnamed x4 -> x1, local copies, waits for them, and re-layouts: 1.7 us -> 0.58 us
    ppermute x1 -> x0, waiting for transfers between devices: 0.83 us -> none  [shards(): lax.ppermute(mine, 'brick', [(source, source ^ 1) for source in range(bri...]
    pallas_call x1, Pallas kernels: 1.36 us -> 0.74 us  [finish(): pl.pallas_call(functools.partial(finish_kernel, bits), out_shape=out, in_...]
    pallas_call x2, Pallas kernels: 3.05 us -> 3.64 us  [the longest x1 2.59 us: pack(): pl.pallas_call(pack_kernel, out_shape=pltpu.VMEM((parts, bricks, depth, L...]
  transfers between devices with their start and end apart: 2 -> 1, of which waited for: 2 -> 1; matrix products, arithmetic and copies ran while one was open for 3% -> 3% of each run, Pallas kernels for 0% -> 0%
where the time goes in v2:
time: 37.8 us; the launch traced here: 37.5 us
  waiting for transfers between devices  11.5 us (30%)
  blocking collectives  10.1 us (27%)
  starting transfers between devices  9.62 us (25%)
  Pallas kernels  4.38 us (12%)
  local copies, waits for them, and re-layouts  1.78 us (5%)
    all_to_all x1, waiting for transfers between devices, shards(): lax.all_to_all(packed, 'brick', 0, 0, axis_index_groups=same_core, tiled=...  11.5 us
    all_gather x1, blocking collectives, shards(): both = lax.all_gather(mine, 'brick', axis_index_groups=same_chip)  10.1 us
    all_to_all x1, starting transfers between devices, shards(): lax.all_to_all(packed, 'brick', 0, 0, axis_index_groups=same_core, tiled=...  9.62 us
    pallas_call x1, Pallas kernels, pack(): pl.pallas_call(pack_kernel, out_shape=pltpu.VMEM((parts, bricks, depth, L...  2.59 us
    slice x1, local copies, waits for them, and re-layouts, shards(): flip = view_rank[:1]  1.2 us
    pallas_call x1, Pallas kernels, composite(): pl.pallas_call(functools.partial(composite_kernel, kappa, depth), out_sha...  1.05 us
  transfers between devices with their start and end apart: 1, of which 1 were waited for; matrix products, arithmetic and copies ran while one was open for 3% of the time, Pallas kernels for 0%

profile of v2, /device:TPU:9, one launch (start us, length us, event | category | flops | bytes accessed | tf_op | source)
XLA Modules:
  0.0 37.5 jit_solution(16432019385404046142)
XLA Ops:
  0.0 2.6 %pack.1 = f32[32,16,2,128]{3,2,1,0:T(2,128)} custom-call(s32[1,16]{1,0:T(1,128)} %owner_hbm.1, f32[16,32,2,128]{3,2,1,0:T(2,128)} %bitcast.8), custom_call_target="tpu_custom_call" | custom-call | tf_op jit(solution)/shard_map/pack/pallas_call | solution.py:38
  2.6 9.6 %all-to-all-start = ((f32[32,16,2,128]{3,2,1,0:T(2,128)}), f32[32,16,2,128]{3,2,1,0:T(2,128)S(1)}, u32[]{:S(2)}, u32[]{:S(2)}) async-start(f32[32,16,2,128]{3,2,1,0:T(2,128)} %pack.1), calls=%async_computation | async-start | bytes 1048576 | tf_op jit(solution)/shard_map/all_to_all | solution.py:129
  12.2 1.2 %slice.3.flip_ref = s32[1]{0:T(128)} slice(s32[1024]{0:T(1024)} %param.5), slice={[0:1]} | slice | bytes 8 | tf_op jit(solution)/shard_map/slice | solution.py:126
  13.4 11.5 %all-to-all-done = f32[32,16,2,128]{3,2,1,0:T(2,128)S(1)} async-done(((f32[32,16,2,128]{3,2,1,0:T(2,128)}), f32[32,16,2,128]{3,2,1,0:T(2,128)S(1)}, u32[]{:S(2)}, u32[]{:S(2)}) %all-to-all-start) | async-done | bytes 524320 | tf_op jit(solution)/shard_map/all_to_all | solution.py:129
  25.0 1.1 %composite.1 = f32[4,16,128]{2,1,0:T(8,128)S(1)} custom-call(s32[1]{0:T(128)} %slice.3.flip_ref, f32[32,32,128]{2,1,0:T(8,128)S(1)} %bitcast.6), custom_call_target="tpu_custom_call" | custom-call | tf_op jit(solution)/shard_map/composite/pallas_call | solution.py:84
  26.0 10.1 %all-gather = f32[8,16,128]{2,1,0:T(8,128)S(1)} all-gather(f32[4,16,128]{2,1,0:T(8,128)S(1)} %composite.1), channel_id=2, replica_groups={{0,16},{32,48},{64,80},{96,112},{128,144},{160,176},{192,208},{224,240}..., dimensions={0}, use_global_device_ids=true | all-gather | bytes 98304 | tf_op jit(solution)/shard_map/all_gather | solution.py:131
  36.2 0.7 %finish.1 = f32[4,1,64]{2,1,0:T(1,128)S(1)} custom-call(s32[1]{0:T(128)} %slice.3.flip_ref, s32[1]{0:T(128)} %bitcast.side_ref, f32[2,4,16,128]{3,2,1,0:T(8,128)S(1)} %bitcast.7), custom_call_target="tpu_custom_call" | custom-call | tf_op jit(solution)/shard_map/finish/pallas_call | solution.py:116
  36.9 0.6 %copy.4 = f32[4,1,64]{2,1,0:T(1,128)} copy(f32[4,1,64]{2,1,0:T(1,128)S(1)} %finish.1) | data formatting | bytes 2048
Async XLA Ops:
  2.6 22.4 %all-to-all-start = ((f32[32,16,2,128]{3,2,1,0:T(2,128)}), f32[32,16,2,128]{3,2,1,0:T(2,128)S(1)}, u32[]{:S(2)}, u32[]{:S(2)}) async-start(f32[32,16,2,128]{3,2,1,0:T(2,128)} %pack.1), calls=%async_computation | async-start | bytes 1048576 | tf_op jit(solution)/shard_map/all_to_all | solution.py:129

commit v3 on v2

v3 whole, which is shorter than its diff:
```python
import functools
import math
import jax
import jax.numpy as jnp
from jax import lax
from jax.experimental import pallas as pl
from jax.experimental.pallas import tpu as pltpu
from jax.sharding import PartitionSpec as P

LANES = 128
VMEM = pl.BlockSpec(memory_space=pltpu.VMEM)
HBM = pl.BlockSpec(memory_space=pltpu.HBM)
PARAMS = pltpu.CompilerParams(vmem_limit_bytes=4 << 20)


def over(front, back):
    keep = front[3]
    return tuple(front[k] + keep * back[k] for k in range(3)) + (keep * back[3],)


def pack_kernel(owner_hbm, ranks_hbm, cells_hbm, out_ref, ranks_ref, owner_ref, owner_sem, ranks_sem, sems):
    bricks = cells_hbm.shape[0]
    fetch = pltpu.make_async_copy(owner_hbm, owner_ref, owner_sem)
    fetch.start()
    ranks = pltpu.make_async_copy(ranks_hbm, ranks_ref, ranks_sem)
    ranks.start()
    fetch.wait()
    copies = [pltpu.make_async_copy(cells_hbm.at[brick], out_ref.at[:, owner_ref[0, brick]], sems.at[brick]) for brick in range(bricks)]
    for copy in copies:
        copy.start()
    for copy in copies:
        copy.wait()
    ranks.wait()


def on_hbm(value):
    return pltpu.with_memory_space_constraint(value, pltpu.HBM)


def pack(owner_map, view_rank, cells):
    bricks, depth, width = cells.shape
    parts = width // LANES
    tiles = cells.reshape(bricks, depth, parts, LANES).transpose(0, 2, 1, 3)
    return pl.pallas_call(
        pack_kernel,
        out_shape=(pltpu.VMEM((parts, bricks, depth, LANES), jnp.float32), pltpu.VMEM((view_rank.size // LANES, LANES), jnp.int32)),
        in_specs=[HBM, HBM, HBM],
        out_specs=(VMEM, VMEM),
        scratch_shapes=[pltpu.SMEM((1, bricks), jnp.int32), pltpu.SemaphoreType.DMA, pltpu.SemaphoreType.DMA, pltpu.SemaphoreType.DMA((bricks,))],
        compiler_params=PARAMS,
        name="pack",
    )(on_hbm(owner_map), on_hbm(view_rank.reshape(-1, LANES)), on_hbm(tiles))


def reverse(value, bits):
    return sum((value >> bit & 1) << (bits - 1 - bit) for bit in range(bits))


def composite_kernel(kappa, depth, ranks_ref, cells_ref, out_ref):
    chips, rows, lanes = cells_ref.shape
    nodes = rows // depth
    bits = chips.bit_length() - 1
    swap = reverse(ranks_ref[0, 0] & (chips - 1), bits)
    scale = -0.125 * math.log2(math.e)
    red = jnp.zeros((nodes, lanes), jnp.float32)
    green = red
    blue = red
    keep = jnp.ones((nodes, lanes), jnp.float32)
    for rank in range(chips):
        chip = reverse(rank, bits) ^ swap
        for slab in range(depth):
            value = cells_ref[chip, pl.ds(slab, nodes, stride=depth), :]
            middle = value * value * scale
            slope = value * (6.0 * scale)
            side = middle + 9.0 * scale
            rest = keep * jnp.exp2(middle * (8.0 * kappa))
            weight = keep - rest
            red = red + weight * jnp.exp2(side + slope)
            green = green + weight * jnp.exp2(middle)
            blue = blue + weight * jnp.exp2(side - slope)
            keep = rest
    out_ref[0] = red
    out_ref[1] = green
    out_ref[2] = blue
    out_ref[3] = keep


def composite(cells, ranks, kappa):
    chips, nodes, depth, lanes = cells.shape
    return pl.pallas_call(
        functools.partial(composite_kernel, kappa, depth),
        out_shape=pltpu.VMEM((4, nodes, lanes), jnp.float32),
        in_specs=[VMEM, VMEM],
        out_specs=VMEM,
        compiler_params=PARAMS,
        name="composite",
    )(ranks, cells.reshape(chips, nodes * depth, lanes))


def finish_kernel(bits, ranks_ref, parts_ref, out_ref):
    nodes, lanes = parts_ref.shape[2:]
    flip = ranks_ref[0, 0]
    node_bits = nodes.bit_length() - 1
    ahead = flip >> (bits - 1 - node_bits) & 1
    total = over(tuple(parts_ref[ahead, k] for k in range(4)), tuple(parts_ref[1 - ahead, k] for k in range(4)))
    for bit in reversed(range(node_bits)):
        half = 1 << bit
        low = tuple(a[:half] for a in total)
        high = tuple(a[half:] for a in total)
        ahead = (flip >> (bits - 1 - bit) & 1) == 0
        front = tuple(jnp.where(ahead, a, b) for a, b in zip(low, high))
        back = tuple(jnp.where(ahead, b, a) for a, b in zip(low, high))
        total = over(front, back)
    first = (lax.axis_index("brick") & 1) == 0
    for k in range(4):
        line = total[k] if k < 3 else 1.0 - total[k]
        out_ref[k] = jnp.where(first, line[:, :lanes // 2], line[:, lanes // 2:])


def finish(parts, ranks, bits):
    out = pltpu.VMEM((4, 1, parts.shape[3] // 2), jnp.float32)
    return pl.pallas_call(functools.partial(finish_kernel, bits), out_shape=out, in_specs=[VMEM, VMEM], out_specs=VMEM, compiler_params=PARAMS, name="finish")(ranks, parts)


def shards(density, owner_map, view_rank):
    nodes = lax.axis_size("node")
    bricks = lax.axis_size("brick")
    kappa = 2.0 / (density.shape[2] * bricks * nodes)
    bits = (bricks * nodes).bit_length() - 1
    same_core = [[2 * chip + core for chip in range(bricks // 2)] for core in range(2)]
    same_chip = [[2 * chip, 2 * chip + 1] for chip in range(bricks // 2)]
    packed, ranks = pack(owner_map, view_rank, density[0])
    cells = lax.all_to_all(packed, "brick", 0, 0, axis_index_groups=same_core, tiled=True)
    mine = composite(cells, ranks, kappa)
    both = lax.all_gather(mine, "brick", axis_index_groups=same_chip)
    return finish(both, ranks, bits)


def solution(mesh):
    in_specs = (P("brick", None, None, "node"), P("brick", None), P())
    out_specs = P(None, "node", "brick")
    return jax.shard_map(shards, mesh=mesh, in_specs=in_specs, out_specs=out_specs, check_vma=False)
```

time: 37.8 us -> 34.8 us (0.921)
  blocking collectives: 10.1 us -> 31.6 us
  waiting for transfers between devices: 11.5 us -> 0 us
  starting transfers between devices: 9.62 us -> 0 us
  Pallas kernels: 4.38 us -> 2.31 us
  local copies, waits for them, and re-layouts: 1.78 us -> 0.58 us
    all_to_all x0 -> x1, blocking collectives: none -> 22 us  [shards(): lax.all_to_all(packed, 'brick', 0, 0, axis_index_groups=same_core, tiled=...]
    all_to_all x1 -> x0, waiting for transfers between devices: 11.5 us -> none  [shards(): lax.all_to_all(packed, 'brick', 0, 0, axis_index_groups=same_core, tiled=...]
    all_to_all x1 -> x0, starting transfers between devices: 9.62 us -> none  [shards(): lax.all_to_all(packed, 'brick', 0, 0, axis_index_groups=same_core, tiled=...]
    slice x1 -> x0, local copies, waits for them, and re-layouts: 1.2 us -> none  [shards(): flip = view_rank[:1]]
    pallas_call x1, Pallas kernels: 2.59 us -> 1.82 us  [pack(): pl.pallas_call(pack_kernel, out_shape=(pltpu.VMEM((parts, bricks, depth,...]
    pallas_call x1, Pallas kernels: 1.05 us -> 0.36 us  [composite(): pl.pallas_call(functools.partial(composite_kernel, kappa, depth), out_sha...]
    pallas_call x1, Pallas kernels: 0.74 us -> 0.13 us  [finish(): pl.pallas_call(functools.partial(finish_kernel, bits), out_shape=out, in_...]
    all_gather x1, blocking collectives: 10.1 us -> 9.62 us  [shards(): both = lax.all_gather(mine, 'brick', axis_index_groups=same_chip)]
  transfers between devices with their start and end apart: 1 -> 0, of which waited for: 1 -> 0; matrix products, arithmetic and copies ran while one was open for 3% -> 0% of each run, Pallas kernels for 0% -> 0%
where the time goes in v3:
time: 34.8 us; the launch traced here: 34.5 us
  blocking collectives  31.6 us (91%)
  Pallas kernels  2.31 us (7%)
  local copies, waits for them, and re-layouts  0.58 us (2%)
    all_to_all x1, blocking collectives, shards(): lax.all_to_all(packed, 'brick', 0, 0, axis_index_groups=same_core, tiled=...  22 us
    all_gather x1, blocking collectives, shards(): both = lax.all_gather(mine, 'brick', axis_index_groups=same_chip)  9.62 us
    pallas_call x1, Pallas kernels, pack(): pl.pallas_call(pack_kernel, out_shape=(pltpu.VMEM((parts, bricks, depth,...  1.82 us

profile of v3, /device:TPU:9, one launch (start us, length us, event | category | flops | bytes accessed | tf_op | source)
XLA Modules:
  0.0 34.5 jit_solution(978978663135255495)
XLA Ops:
  0.0 1.8 %pack.1 = (f32[32,16,2,128]{3,2,1,0:T(2,128)S(1)}, s32[8,128]{1,0:T(8,128)S(1)}) custom-call(s32[1,16]{1,0:T(1,128)} %owner_hbm.1, s32[8,128]{1,0:T(8,128)} %bitcast.9, f32[16,32,2,128]{3,2,1,0:T(2,128)} %bitcast.8), custom_call_target="tpu_custom_call" | custom-call | tf_op jit(solution)/shard_map/pack/pallas_call | solution.py:44
  1.8 22.0 %all_to_all.5 = f32[32,16,2,128]{3,2,1,0:T(2,128)S(1)} all-to-all(f32[32,16,2,128]{3,2,1,0:T(2,128)S(1)} %get-tuple-element.8), channel_id=1, replica_groups={{0,32,64,96,128,160,192,224,256,288,320,352,384,416,448,480,512,544,576..., dimensions={0} | all-to-all | bytes 1048576 | tf_op jit(solution)/shard_map/all_to_all | solution.py:133
  23.8 0.4 %composite.1 = f32[4,16,128]{2,1,0:T(8,128)S(1)} custom-call(s32[8,128]{1,0:T(8,128)S(1)} %get-tuple-element.7.ranks_ref, f32[32,32,128]{2,1,0:T(8,128)S(1)} %bitcast.6), custom_call_target="tpu_custom_call" | custom-call | tf_op jit(solution)/shard_map/composite/pallas_call | solution.py:90
  24.2 9.6 %all-gather = f32[8,16,128]{2,1,0:T(8,128)S(1)} all-gather(f32[4,16,128]{2,1,0:T(8,128)S(1)} %composite.1), channel_id=2, replica_groups={{0,16},{32,48},{64,80},{96,112},{128,144},{160,176},{192,208},{224,240}..., dimensions={0}, use_global_device_ids=true | all-gather | bytes 98304 | tf_op jit(solution)/shard_map/all_gather | solution.py:135
  33.8 0.1 finish.1
  33.9 0.6 %copy.4 = f32[4,1,64]{2,1,0:T(1,128)} copy(f32[4,1,64]{2,1,0:T(1,128)S(1)} %finish.1) | data formatting | bytes 2048

commit v4 on v3

--- a/solution.py
+++ b/solution.py
@@ -8,6 +8,18 @@
 from jax.sharding import PartitionSpec as P
 
 LANES = 128
+ACROSS, ALONG = 4, 8
+
+
+def chip_at(place):
+    step, along = place // ALONG, place % ALONG
+    return (step + along) % ACROSS * ALONG + along
+
+
+def place_of(chip):
+    return ((chip >> ALONG.bit_length() - 1) - chip & ACROSS - 1) * ALONG + (chip & ALONG - 1)
+
+
 VMEM = pl.BlockSpec(memory_space=pltpu.VMEM)
 HBM = pl.BlockSpec(memory_space=pltpu.HBM)
 PARAMS = pltpu.CompilerParams(vmem_limit_bytes=4 << 20)
@@ -18,18 +30,21 @@
     return tuple(front[k] + keep * back[k] for k in range(3)) + (keep * back[3],)
 
 
-def pack_kernel(owner_hbm, ranks_hbm, cells_hbm, out_ref, ranks_ref, owner_ref, owner_sem, ranks_sem, sems):
+def pack_kernel(owner_hbm, ranks_hbm, cells_hbm, out_ref, ranks_ref, owner_ref, staged_ref, owner_sem, ranks_sem, sems):
     bricks = cells_hbm.shape[0]
-    fetch = pltpu.make_async_copy(owner_hbm, owner_ref, owner_sem)
-    fetch.start()
+    owner = pltpu.make_async_copy(owner_hbm, owner_ref, owner_sem)
+    owner.start()
+    copies = [pltpu.make_async_copy(cells_hbm.at[brick], staged_ref.at[brick], sems.at[brick]) for brick in range(bricks)]
+    for copy in copies:
+        copy.start()
     ranks = pltpu.make_async_copy(ranks_hbm, ranks_ref, ranks_sem)
     ranks.start()
-    fetch.wait()
-    copies = [pltpu.make_async_copy(cells_hbm.at[brick], out_ref.at[:, owner_ref[0, brick]], sems.at[brick]) for brick in range(bricks)]
-    for copy in copies:
-        copy.start()
-    for copy in copies:
-        copy.wait()
+    owner.wait()
+    for brick in range(bricks):
+        copies[brick].wait()
+        slot = owner_ref[0, brick]
+        for place in range(out_ref.shape[0]):
+            out_ref[place, slot] = staged_ref[brick, chip_at(place)]
     ranks.wait()
 
 
@@ -46,7 +61,7 @@
         out_shape=(pltpu.VMEM((parts, bricks, depth, LANES), jnp.float32), pltpu.VMEM((view_rank.size // LANES, LANES), jnp.int32)),
         in_specs=[HBM, HBM, HBM],
         out_specs=(VMEM, VMEM),
-        scratch_shapes=[pltpu.SMEM((1, bricks), jnp.int32), pltpu.SemaphoreType.DMA, pltpu.SemaphoreType.DMA, pltpu.SemaphoreType.DMA((bricks,))],
+        scratch_shapes=[pltpu.SMEM((1, bricks), jnp.int32), pltpu.VMEM((bricks, parts, depth, LANES), jnp.float32), pltpu.SemaphoreType.DMA, pltpu.SemaphoreType.DMA, pltpu.SemaphoreType.DMA((bricks,))],
         compiler_params=PARAMS,
         name="pack",
     )(on_hbm(owner_map), on_hbm(view_rank.reshape(-1, LANES)), on_hbm(tiles))
@@ -67,9 +82,9 @@
     blue = red
     keep = jnp.ones((nodes, lanes), jnp.float32)
     for rank in range(chips):
-        chip = reverse(rank, bits) ^ swap
+        place = place_of(reverse(rank, bits) ^ swap)
         for slab in range(depth):
-            value = cells_ref[chip, pl.ds(slab, nodes, stride=depth), :]
+            value = cells_ref[place, pl.ds(slab, nodes, stride=depth), :]
             middle = value * value * scale
             slope = value * (6.0 * scale)
             side = middle + 9.0 * scale
@@ -127,7 +142,7 @@
     bricks = lax.axis_size("brick")
     kappa = 2.0 / (density.shape[2] * bricks * nodes)
     bits = (bricks * nodes).bit_length() - 1
-    same_core = [[2 * chip + core for chip in range(bricks // 2)] for core in range(2)]
+    same_core = [[2 * chip + core for chip in map(chip_at, range(bricks // 2))] for core in range(2)]
     same_chip = [[2 * chip, 2 * chip + 1] for chip in range(bricks // 2)]
     packed, ranks = pack(owner_map, view_rank, density[0])
     cells = lax.all_to_all(packed, "brick", 0, 0, axis_index_groups=same_core, tiled=True)

time: 34.8 us -> 34.2 us (0.983)
  the two profiles are of different devices: /device:TPU:9 before, /device:TPU:1 now
where the time goes in v4:
time: 34.2 us; the launch traced here: 33.9 us
  blocking collectives  31.6 us (92%)
  Pallas kernels  1.78 us (5%)
  local copies, waits for them, and re-layouts  0.58 us (2%)
    all_to_all x1, blocking collectives, shards(): lax.all_to_all(packed, 'brick', 0, 0, axis_index_groups=same_core, tiled=...  22.2 us
    all_gather x1, blocking collectives, shards(): both = lax.all_gather(mine, 'brick', axis_index_groups=same_chip)  9.4 us
    pallas_call x1, Pallas kernels, pack(): pl.pallas_call(pack_kernel, out_shape=(pltpu.VMEM((parts, bricks, depth,...  1.28 us

profile of v4, /device:TPU:1, one launch (start us, length us, event | category | flops | bytes accessed | tf_op | source)
XLA Modules:
  0.0 33.9 jit_solution(3522174697641187454)
XLA Ops:
  0.0 1.3 %pack.1 = (f32[32,16,2,128]{3,2,1,0:T(2,128)S(1)}, s32[8,128]{1,0:T(8,128)S(1)}) custom-call(s32[1,16]{1,0:T(1,128)} %owner_hbm.1, s32[8,128]{1,0:T(8,128)} %bitcast.9, f32[16,32,2,128]{3,2,1,0:T(2,128)} %bitcast.8), custom_call_target="tpu_custom_call" | custom-call | tf_op jit(solution)/shard_map/pack/pallas_call | solution.py:59
  1.3 22.2 %all_to_all.5 = f32[32,16,2,128]{3,2,1,0:T(2,128)S(1)} all-to-all(f32[32,16,2,128]{3,2,1,0:T(2,128)S(1)} %get-tuple-element.8), channel_id=1, replica_groups={{0,288,576,864,128,416,704,992,256,544,832,96,384,672,960,224,512,800,6..., dimensions={0} | all-to-all | bytes 1048576 | tf_op jit(solution)/shard_map/all_to_all | solution.py:148
  23.5 0.4 %composite.1 = f32[4,16,128]{2,1,0:T(8,128)S(1)} custom-call(s32[8,128]{1,0:T(8,128)S(1)} %get-tuple-element.7.ranks_ref, f32[32,32,128]{2,1,0:T(8,128)S(1)} %bitcast.6), custom_call_target="tpu_custom_call" | custom-call | tf_op jit(solution)/shard_map/composite/pallas_call | solution.py:105
  23.8 9.4 %all-gather = f32[8,16,128]{2,1,0:T(8,128)S(1)} all-gather(f32[4,16,128]{2,1,0:T(8,128)S(1)} %composite.1), channel_id=2, replica_groups={{0,16},{32,48},{64,80},{96,112},{128,144},{160,176},{192,208},{224,240}..., dimensions={0}, use_global_device_ids=true | all-gather | bytes 98304 | tf_op jit(solution)/shard_map/all_gather | solution.py:150
  33.2 0.1 finish.1
  33.4 0.6 %copy.4 = f32[4,1,64]{2,1,0:T(1,128)} copy(f32[4,1,64]{2,1,0:T(1,128)S(1)} %finish.1) | data formatting | bytes 2048

commit v5 on v4

--- a/solution.py
+++ b/solution.py
@@ -12,12 +12,14 @@
 
 
 def chip_at(place):
-    step, along = place // ALONG, place % ALONG
-    return (step + along) % ACROSS * ALONG + along
+    step, turn = place // ALONG, place % ALONG
+    return (step + 1 + turn) % ACROSS * ALONG + -turn % ALONG
 
 
 def place_of(chip):
-    return ((chip >> ALONG.bit_length() - 1) - chip & ACROSS - 1) * ALONG + (chip & ALONG - 1)
+    turn = -chip & ALONG - 1
+    step = (chip >> ALONG.bit_length() - 1) - 1 - turn & ACROSS - 1
+    return step * ALONG + turn
 
 
 VMEM = pl.BlockSpec(memory_space=pltpu.VMEM)

time: 34.2 us -> 33 us (0.965)
  the two profiles are of different devices: /device:TPU:1 before, /device:TPU:17 now
where the time goes in v5:
time: 33 us; the launch traced here: 32.8 us
  blocking collectives  30.4 us (92%)
  Pallas kernels  1.78 us (5%)
  local copies, waits for them, and re-layouts  0.58 us (2%)
    all_to_all x1, blocking collectives, shards(): lax.all_to_all(packed, 'brick', 0, 0, axis_index_groups=same_core, tiled=...  21 us
    all_gather x1, blocking collectives, shards(): both = lax.all_gather(mine, 'brick', axis_index_groups=same_chip)  9.38 us
    pallas_call x1, Pallas kernels, pack(): pl.pallas_call(pack_kernel, out_shape=(pltpu.VMEM((parts, bricks, depth,...  1.28 us

profile of v5, /device:TPU:17, one launch (start us, length us, event | category | flops | bytes accessed | tf_op | source)
XLA Modules:
  0.0 32.8 jit_solution(18202246037120320557)
XLA Ops:
  0.0 1.3 %pack.1 = (f32[32,16,2,128]{3,2,1,0:T(2,128)S(1)}, s32[8,128]{1,0:T(8,128)S(1)}) custom-call(s32[1,16]{1,0:T(1,128)} %owner_hbm.1, s32[8,128]{1,0:T(8,128)} %bitcast.9, f32[16,32,2,128]{3,2,1,0:T(2,128)} %bitcast.8), custom_call_target="tpu_custom_call" | custom-call | tf_op jit(solution)/shard_map/pack/pallas_call | solution.py:61
  1.3 21.0 %all_to_all.5 = f32[32,16,2,128]{3,2,1,0:T(2,128)S(1)} all-to-all(f32[32,16,2,128]{3,2,1,0:T(2,128)S(1)} %get-tuple-element.8), channel_id=1, replica_groups={{256,736,960,160,384,608,832,32,512,992,192,416,640,864,64,288,768,224,..., dimensions={0} | all-to-all | bytes 1048576 | tf_op jit(solution)/shard_map/all_to_all | solution.py:150
  22.3 0.4 %composite.1 = f32[4,16,128]{2,1,0:T(8,128)S(1)} custom-call(s32[8,128]{1,0:T(8,128)S(1)} %get-tuple-element.7.ranks_ref, f32[32,32,128]{2,1,0:T(8,128)S(1)} %bitcast.6), custom_call_target="tpu_custom_call" | custom-call | tf_op jit(solution)/shard_map/composite/pallas_call | solution.py:107
  22.7 9.4 %all-gather = f32[8,16,128]{2,1,0:T(8,128)S(1)} all-gather(f32[4,16,128]{2,1,0:T(8,128)S(1)} %composite.1), channel_id=2, replica_groups={{0,16},{32,48},{64,80},{96,112},{128,144},{160,176},{192,208},{224,240}..., dimensions={0}, use_global_device_ids=true | all-gather | bytes 98304 | tf_op jit(solution)/shard_map/all_gather | solution.py:152
  32.1 0.1 finish.1
  32.2 0.6 %copy.4 = f32[4,1,64]{2,1,0:T(1,128)} copy(f32[4,1,64]{2,1,0:T(1,128)S(1)} %finish.1) | data formatting | bytes 2048

commit v6 on v5

--- a/solution.py
+++ b/solution.py
@@ -11,14 +11,19 @@
 ACROSS, ALONG = 4, 8
 
 
+SHIFTS = (1, 0, 3, 0, 1, 2, 0, 1)
+TABLE = sum(shift << 2 * turn for turn, shift in enumerate(SHIFTS))
+
+
 def chip_at(place):
     step, turn = place // ALONG, place % ALONG
-    return (step + 1 + turn) % ACROSS * ALONG + -turn % ALONG
+    return (step + SHIFTS[turn]) % ACROSS * ALONG + -turn % ALONG
 
 
 def place_of(chip):
     turn = -chip & ALONG - 1
-    step = (chip >> ALONG.bit_length() - 1) - 1 - turn & ACROSS - 1
+    shift = jnp.int32(TABLE) >> 2 * turn
+    step = (chip >> ALONG.bit_length() - 1) - shift & ACROSS - 1
     return step * ALONG + turn
 
 

time: 33 us -> 32.3 us (0.979)
  the two profiles are of different devices: /device:TPU:17 before, /device:TPU:9 now
where the time goes in v6:
time: 32.3 us; the launch traced here: 32.1 us
  blocking collectives  29.7 us (92%)
  Pallas kernels  1.78 us (6%)
  local copies, waits for them, and re-layouts  0.58 us (2%)
    all_to_all x1, blocking collectives, shards(): lax.all_to_all(packed, 'brick', 0, 0, axis_index_groups=same_core, tiled=...  20.4 us
    all_gather x1, blocking collectives, shards(): both = lax.all_gather(mine, 'brick', axis_index_groups=same_chip)  9.35 us
    pallas_call x1, Pallas kernels, pack(): pl.pallas_call(pack_kernel, out_shape=(pltpu.VMEM((parts, bricks, depth,...  1.28 us

profile of v6, /device:TPU:9, one launch (start us, length us, event | category | flops | bytes accessed | tf_op | source)
XLA Modules:
  0.0 32.1 jit_solution(977897087707927843)
XLA Ops:
  0.0 1.3 %pack.1 = (f32[32,16,2,128]{3,2,1,0:T(2,128)S(1)}, s32[8,128]{1,0:T(8,128)S(1)}) custom-call(s32[1,16]{1,0:T(1,128)} %owner_hbm.1, s32[8,128]{1,0:T(8,128)} %bitcast.9, f32[16,32,2,128]{3,2,1,0:T(2,128)} %bitcast.8), custom_call_target="tpu_custom_call" | custom-call | tf_op jit(solution)/shard_map/pack/pallas_call | solution.py:66
  1.3 20.4 %all_to_all.5 = f32[32,16,2,128]{3,2,1,0:T(2,128)S(1)} all-to-all(f32[32,16,2,128]{3,2,1,0:T(2,128)S(1)} %get-tuple-element.8), channel_id=1, replica_groups={{256,224,960,160,384,608,64,288,512,480,192,416,640,864,320,544,768,736..., dimensions={0} | all-to-all | bytes 1048576 | tf_op jit(solution)/shard_map/all_to_all | solution.py:155
  21.7 0.4 %composite.1 = f32[4,16,128]{2,1,0:T(8,128)S(1)} custom-call(s32[8,128]{1,0:T(8,128)S(1)} %get-tuple-element.7.ranks_ref, f32[32,32,128]{2,1,0:T(8,128)S(1)} %bitcast.6), custom_call_target="tpu_custom_call" | custom-call | tf_op jit(solution)/shard_map/composite/pallas_call | solution.py:112
  22.0 9.4 %all-gather = f32[8,16,128]{2,1,0:T(8,128)S(1)} all-gather(f32[4,16,128]{2,1,0:T(8,128)S(1)} %composite.1), channel_id=2, replica_groups={{0,16},{32,48},{64,80},{96,112},{128,144},{160,176},{192,208},{224,240}..., dimensions={0}, use_global_device_ids=true | all-gather | bytes 98304 | tf_op jit(solution)/shard_map/all_gather | solution.py:157
  31.4 0.1 finish.1
  31.5 0.6 %copy.4 = f32[4,1,64]{2,1,0:T(1,128)} copy(f32[4,1,64]{2,1,0:T(1,128)S(1)} %finish.1) | data formatting | bytes 2048

commit v7 on v6

--- a/solution.py
+++ b/solution.py
@@ -11,7 +11,7 @@
 ACROSS, ALONG = 4, 8
 
 
-SHIFTS = (1, 0, 3, 0, 1, 2, 0, 1)
+SHIFTS = (1, 1, 3, 0, 1, 3, 0, 1)
 TABLE = sum(shift << 2 * turn for turn, shift in enumerate(SHIFTS))
 
 

time: 32.3 us -> 32.2 us (level)
  the two profiles are of different devices: /device:TPU:9 before, /device:TPU:1 now
where the time goes in v7:
time: 32.2 us; the launch traced here: 32 us
  blocking collectives  29.6 us (92%)
  Pallas kernels  1.78 us (6%)
  local copies, waits for them, and re-layouts  0.58 us (2%)
    all_to_all x1, blocking collectives, shards(): lax.all_to_all(packed, 'brick', 0, 0, axis_index_groups=same_core, tiled=...  20.3 us
    all_gather x1, blocking collectives, shards(): both = lax.all_gather(mine, 'brick', axis_index_groups=same_chip)  9.34 us
    pallas_call x1, Pallas kernels, pack(): pl.pallas_call(pack_kernel, out_shape=(pltpu.VMEM((parts, bricks, depth,...  1.28 us

profile of v7, /device:TPU:1, one launch (start us, length us, event | category | flops | bytes accessed | tf_op | source)
XLA Modules:
  0.0 32.0 jit_solution(14476704535046977385)
XLA Ops:
  0.0 1.3 %pack.1 = (f32[32,16,2,128]{3,2,1,0:T(2,128)S(1)}, s32[8,128]{1,0:T(8,128)S(1)}) custom-call(s32[1,16]{1,0:T(1,128)} %owner_hbm.1, s32[8,128]{1,0:T(8,128)} %bitcast.9, f32[16,32,2,128]{3,2,1,0:T(2,128)} %bitcast.8), custom_call_target="tpu_custom_call" | custom-call | tf_op jit(solution)/shard_map/pack/pallas_call | solution.py:66
  1.3 20.3 %all_to_all.5 = f32[32,16,2,128]{3,2,1,0:T(2,128)S(1)} all-to-all(f32[32,16,2,128]{3,2,1,0:T(2,128)S(1)} %get-tuple-element.8), channel_id=1, replica_groups={{256,480,960,160,384,864,64,288,512,736,192,416,640,96,320,544,768,992,..., dimensions={0} | all-to-all | bytes 1048576 | tf_op jit(solution)/shard_map/all_to_all | solution.py:155
  21.6 0.4 %composite.1 = f32[4,16,128]{2,1,0:T(8,128)S(1)} custom-call(s32[8,128]{1,0:T(8,128)S(1)} %get-tuple-element.7.ranks_ref, f32[32,32,128]{2,1,0:T(8,128)S(1)} %bitcast.6), custom_call_target="tpu_custom_call" | custom-call | tf_op jit(solution)/shard_map/composite/pallas_call | solution.py:112
  22.0 9.3 %all-gather = f32[8,16,128]{2,1,0:T(8,128)S(1)} all-gather(f32[4,16,128]{2,1,0:T(8,128)S(1)} %composite.1), channel_id=2, replica_groups={{0,16},{32,48},{64,80},{96,112},{128,144},{160,176},{192,208},{224,240}..., dimensions={0}, use_global_device_ids=true | all-gather | bytes 98304 | tf_op jit(solution)/shard_map/all_gather | solution.py:157
  31.3 0.1 finish.1
  31.4 0.6 %copy.4 = f32[4,1,64]{2,1,0:T(1,128)} copy(f32[4,1,64]{2,1,0:T(1,128)S(1)} %finish.1) | data formatting | bytes 2048
